TPU v7x, 32 devices: a whole 2x2x4 slice. The times are simulated.
32 devices in a mesh: vessel: 2 (over core), gather: 16 (over z, y, x).
Axes of the slice: x: 2, y: 2, z: 4, core: 2. Of those that a mesh axis runs over, the one named last changes fastest.
Arguments:
- observed: bfloat16 [16, 16, 2048], P('gather'), may hold values from -6 to 6
- estimate: bfloat16 [2, 16, 16, 2048], P('vessel', 'gather'), may hold values from -6 to 6
- delays: int32 [2, 16], P('vessel', 'gather'), may hold values from 0 to 256
- taps_time: float32 [16, 7], replicated, may hold values from -2 to 2
- taps_shot: float32 [16, 7], replicated, may hold values from -0.5 to 0.5
- thresh: float32 [16], replicated, may hold values from 0.02 to 0.3
Outputs:
- deblended: bfloat16 [2, 16, 16, 2048], P('vessel', 'gather')
All inputs are finite; a program needn't handle non-finite values.
Results may differ from a plain program's by a relative error of at most 0.022.
Values may be sent and summed in bfloat16 or wider, within the bound.
A program may use at most 64 MiB of HBM per device.

v0:
```python
import jax
import jax.numpy as jnp
from jax import lax
from jax.sharding import PartitionSpec as P

TIME_SPACING = 4
SHOT_SPACING = 2
MAXD = 256
ITERS = 2


def late_shift(traces, shift_by):
    width = traces.shape[2]
    padded = jnp.pad(traces, ((0, 0), (0, 0), (MAXD, MAXD)))

    def late_single(trace, shift_amount):
        return lax.dynamic_slice_in_dim(trace, MAXD - shift_amount, width, 1)

    return jax.vmap(late_single)(padded, shift_by)


def early_shift(traces, shift_by):
    width = traces.shape[2]
    padded = jnp.pad(traces, ((0, 0), (0, 0), (MAXD, MAXD)))

    def early_single(trace, shift_amount):
        return lax.dynamic_slice_in_dim(trace, MAXD + shift_amount, width, 1)

    return jax.vmap(early_single)(padded, shift_by)


def along_time(field, taps, shift_sign):
    filter_reach = 3 * TIME_SPACING
    length = field.shape[3]
    padded = jnp.pad(field, ((0, 0), (0, 0), (0, 0), (filter_reach, filter_reach)))
    total = jnp.zeros((taps.shape[0],) + field.shape[1:], jnp.float32)
    for tap_index in range(-3, 4):
        start_offset = filter_reach + shift_sign * tap_index * TIME_SPACING
        total = (
            total
            + taps[:, tap_index + 3][:, None, None, None]
            * padded[:, :, :, start_offset : start_offset + length]
        )
    return total


def along_shots(field, taps, shift_sign):
    filter_reach = 3 * SHOT_SPACING
    length = field.shape[1]
    padded = jnp.pad(field, ((0, 0), (filter_reach, filter_reach), (0, 0), (0, 0)))
    total = jnp.zeros((taps.shape[0],) + field.shape[1:], jnp.float32)
    for tap_index in range(-3, 4):
        start_offset = filter_reach + shift_sign * tap_index * SHOT_SPACING
        total = (
            total
            + taps[:, tap_index + 3][:, None, None, None]
            * padded[:, start_offset : start_offset + length]
        )
    return total


def shrink_filter(plane, taps_time, taps_shot, thresh):
    field = plane.astype(jnp.float32)[None]
    group_time = taps_time.reshape(-1, 4, taps_time.shape[1])
    group_shot = taps_shot.reshape(-1, 4, taps_shot.shape[1])
    group_thresh = thresh.reshape(-1, 4)

    def channel(carry, pieces):
        time_taps, shot_taps, limits = pieces
        forward_pass = along_shots(along_time(field, time_taps, 1), shot_taps, 1)
        bound = limits[:, None, None, None]
        shrunk = forward_pass - jnp.clip(forward_pass, -bound, bound)
        back = along_time(along_shots(shrunk, shot_taps, -1), time_taps, -1)
        return (carry + jnp.sum(back, axis=0), None)

    total, _ = lax.scan(
        channel, jnp.zeros(plane.shape, jnp.float32), (group_time, group_shot, group_thresh)
    )
    return total.astype(jnp.bfloat16)


def pseudo_planes(current, observed, shot_delays):
    own = late_shift(current[0], shot_delays[0])
    blend = lax.psum(own, "vessel").astype(jnp.float32)
    resid = observed.astype(jnp.float32) - blend
    plane = current[0].astype(jnp.float32) + early_shift(resid, shot_delays[0])
    return plane.astype(jnp.bfloat16)[None]


def per_device(observed, estimate, delays, taps_time, taps_shot, thresh):
    current = estimate
    for step in range(ITERS):
        planes = pseudo_planes(current, observed, delays)
        filtered = jnp.stack(
            [
                shrink_filter(
                    lax.all_to_all(planes, "gather", split_axis=2, concat_axis=1, tiled=True)[0],
                    taps_time,
                    taps_shot,
                    thresh,
                )
            ]
        )
        current = lax.all_to_all(filtered, "gather", split_axis=1, concat_axis=2, tiled=True)
    return current


def solution(mesh):
    return jax.shard_map(
        per_device,
        mesh=mesh,
        in_specs=(
            P("gather", None, None),
            P("vessel", "gather", None, None),
            P("vessel", "gather"),
            P(),
            P(),
            P(),
        ),
        out_specs=P("vessel", "gather", None, None),
        check_vma=False,
    )
```

profile of v0, /device:TPU:0, one launch (start us, length us, event | category | flops | bytes accessed | tf_op | source)
XLA Modules:
  0.0 136.3 jit_solution(2640347895954889670)
XLA Ops:
  7.2 1.6 %pad_dynamic-slice_fusion.3 = bf16[1,16,2048]{2,1,0:T(8,128)(2,1)} fusion(s32[]{:T(128)} %bitcast.5, bf16[1,16,2048]{2,1,0:T(8,128)(2,1)} %bitcast.111), kind=kLoop, calls=%fused_computation.150 | loop fusion | bytes 131076 | tf_op jit(solution)/shard_map/vmap()/gather | solution.py:17
  8.8 21.3 %all-reduce.15.cloned.1.call-done = bf16[1,16,2048]{2,1,0:T(8,128)(2,1)} async-done(((bf16[1,16,2048]{2,1,0:T(8,128)(2,1)}), bf16[1,16,2048]{2,1,0:T(8,128)(2,1)}) %all-reduce.15.cloned.1.call-update) | async-done | bytes 65552 | tf_op jit(solution)/shard_map/psum | solution.py:84
  30.1 0.9 convert_subtract_fusion.1
  31.1 0.7 copy-done
  31.9 0.5 broadcast.734
  32.5 1.0 reduce.64
  33.5 0.7 reshape.633
  34.1 7.0 %all-to-all-start = ((bf16[16,2,1024]{2,1,0:T(2,128)(2,1)}), bf16[16,2,1024]{2,1,0:T(2,128)(2,1)S(1)}, u32[]{:S(2)}, u32[]{:S(2)}) async-start(bf16[16,2,1024]{2,1,0:T(2,128)(2,1)} %reshape.633), calls=%async_computation | async-start | bytes 131072 | tf_op jit(solution)/shard_map/all_to_all | solution.py:97
  41.2 0.6 copy-done.3
  41.9 0.6 copy-done.4
  42.6 6.0 %all-to-all-done = bf16[16,2,1024]{2,1,0:T(2,128)(2,1)S(1)} async-done(((bf16[16,2,1024]{2,1,0:T(2,128)(2,1)}), bf16[16,2,1024]{2,1,0:T(2,128)(2,1)S(1)}, u32[]{:S(2)}, u32[]{:S(2)}) %all-to-all-start) | async-done | bytes 65568 | tf_op jit(solution)/shard_map/all_to_all | solution.py:97
  48.9 12.3 %while.30 = (s32[]{:T(128)}, f32[16,1,2048]{2,0,1:T(8,128)S(1)}, f32[4,4,7]{2,1,0:T(4,128)S(1)}, f32[4,4,7]{2,1,0:T(4,128)S(1)}, f32[1,16,1,2048]{3,1,2,0:T(8,12...) while((s32[]{:T(128)}, f32[16,1,2048]{2,0,1:T(8,128)S(1)}, f32[4,4,7]{2,1,0:T(4,128)S(1)}, ...), condition=%wide.region_3.4_spmd.clone, body=%wide.region_1.3_spmd.clone.sunk | while | flops 7372807 | bytes 5506551 | solution.py:76
  50.0 0.5 minimum_subtract_fusion.4
  50.5 0.4 fusion.70
  51.0 0.9 add_reduce_fusion.4
  53.1 0.5 minimum_subtract_fusion.4
  53.6 0.4 fusion.70
  54.0 0.9 add_reduce_fusion.4
  56.1 0.5 minimum_subtract_fusion.4
  56.6 0.4 fusion.70
  57.1 0.9 add_reduce_fusion.4
  59.2 0.5 minimum_subtract_fusion.4
  60.2 0.9 add_reduce_fusion.4
  61.2 1.0 reduce.65
  62.2 10.1 %all_to_all.19 = bf16[16,2,1024]{2,1,0:T(2,128)(2,1)S(1)} all-to-all(bf16[16,2,1024]{2,1,0:T(2,128)(2,1)S(1)} %reshape.635), channel_id=1, replica_groups=mesh['vessel'=2,'gather'=16] {'gather'}, dimensions={0} | all-to-all | bytes 131072 | tf_op jit(solution)/shard_map/all_to_all | solution.py:104
  72.5 0.7 pad_dynamic-slice_fusion.2
  73.2 14.6 %all-reduce.17.cloned.1.call-done = bf16[1,16,2048]{2,1,0:T(8,128)(2,1)} async-done(((bf16[1,16,2048]{2,1,0:T(8,128)(2,1)}), bf16[1,16,2048]{2,1,0:T(8,128)(2,1)}) %all-reduce.17.cloned.1.call-update) | async-done | bytes 65552 | tf_op jit(solution)/shard_map/psum | solution.py:84
  87.8 0.9 convert_subtract_fusion
  89.0 1.0 reduce.66
  89.9 0.7 reshape.637
  90.6 6.8 %all-to-all-start.2 = ((bf16[16,2,1024]{2,1,0:T(2,128)(2,1)}), bf16[16,2,1024]{2,1,0:T(2,128)(2,1)S(1)}, u32[]{:S(2)}, u32[]{:S(2)}) async-start(bf16[16,2,1024]{2,1,0:T(2,128)(2,1)} %reshape.637), calls=%async_computation.2 | async-start | bytes 131072 | tf_op jit(solution)/shard_map/all_to_all | solution.py:97
  97.4 7.5 %all-to-all-done.2 = bf16[16,2,1024]{2,1,0:T(2,128)(2,1)S(1)} async-done(((bf16[16,2,1024]{2,1,0:T(2,128)(2,1)}), bf16[16,2,1024]{2,1,0:T(2,128)(2,1)S(1)}, u32[]{:S(2)}, u32[]{:S(2)}) %all-to-all-start.2) | async-done | bytes 65568 | tf_op jit(solution)/shard_map/all_to_all | solution.py:97
  105.2 12.3 %while.31 = (s32[]{:T(128)}, f32[16,1,2048]{2,0,1:T(8,128)S(1)}, f32[4,4,7]{2,1,0:T(4,128)S(1)}, f32[4,4,7]{2,1,0:T(4,128)S(1)}, f32[1,16,1,2048]{3,1,2,0:T(8,12...) while((s32[]{:T(128)}, f32[16,1,2048]{2,0,1:T(8,128)S(1)}, f32[4,4,7]{2,1,0:T(4,128)S(1)}, ...), condition=%wide.region_7.8_spmd.clone, body=%wide.region_5.7_spmd.clone.sunk | while | flops 7372807 | bytes 5506551 | solution.py:76
  106.3 0.5 minimum_subtract_fusion.5
  106.9 0.4 fusion.72
  107.3 0.9 add_reduce_fusion.5
  109.4 0.5 minimum_subtract_fusion.5
  109.9 0.4 fusion.72
  110.4 0.9 add_reduce_fusion.5
  112.5 0.5 minimum_subtract_fusion.5
  113.0 0.4 fusion.72
  113.4 0.9 add_reduce_fusion.5
  115.5 0.5 minimum_subtract_fusion.5
  116.1 0.4 fusion.72
  116.5 0.9 add_reduce_fusion.5
  117.6 1.0 reduce.67
  118.6 10.1 %all_to_all.40 = bf16[16,2,1024]{2,1,0:T(2,128)(2,1)S(1)} all-to-all(bf16[16,2,1024]{2,1,0:T(2,128)(2,1)S(1)} %reshape.639), channel_id=1, replica_groups=mesh['vessel'=2,'gather'=16] {'gather'}, dimensions={0} | all-to-all | bytes 131072 | tf_op jit(solution)/shard_map/all_to_all | solution.py:104
  128.8 0.7 copy.50
  (92 shorter events, 11.3 us)
Async XLA Ops:
  6.5 23.6 %all-reduce.15.cloned.1.call-start = ((), (), s32[]{:S(2)}) async-start(), calls=%async_computation.4 | async-start | bytes 131072 | tf_op jit(solution)/shard_map/psum | solution.py:84
  8.8 21.3 %copy-start.1 = (bf16[1,16,2048]{2,1,0:T(8,128)(2,1)S(1)}, bf16[1,16,2048]{2,1,0:T(8,128)(2,1)}, u32[]{:S(2)}) copy-start(bf16[1,16,2048]{2,1,0:T(8,128)(2,1)} %param.10) | copy-start | bytes 196612
  31.0 0.8 copy-start
  34.1 7.0 %copy-start.2 = (f32[16,7]{0,1:T(8,128)S(1)}, f32[16,7]{0,1:T(8,128)}, u32[]{:S(2)}) copy-start(f32[16,7]{0,1:T(8,128)} %param.13) | copy-start | bytes 1348
  34.1 14.5 %all-to-all-start = ((bf16[16,2,1024]{2,1,0:T(2,128)(2,1)}), bf16[16,2,1024]{2,1,0:T(2,128)(2,1)S(1)}, u32[]{:S(2)}, u32[]{:S(2)}) async-start(bf16[16,2,1024]{2,1,0:T(2,128)(2,1)} %reshape.633), calls=%async_computation | async-start | bytes 131072 | tf_op jit(solution)/shard_map/all_to_all | solution.py:97
  41.1 46.7 %all-reduce.17.cloned.1.call-start = ((), (), s32[]{:S(2)}) async-start(), calls=%async_computation.5 | async-start | bytes 131072 | tf_op jit(solution)/shard_map/psum | solution.py:84
  41.2 0.7 copy-start.3
  41.8 0.7 copy-start.4
  90.6 14.4 %all-to-all-start.2 = ((bf16[16,2,1024]{2,1,0:T(2,128)(2,1)}), bf16[16,2,1024]{2,1,0:T(2,128)(2,1)S(1)}, u32[]{:S(2)}, u32[]{:S(2)}) async-start(bf16[16,2,1024]{2,1,0:T(2,128)(2,1)} %reshape.637), calls=%async_computation.2 | async-start | bytes 131072 | tf_op jit(solution)/shard_map/all_to_all | solution.py:97
Sparse Core Ops, SparseCore 0:
  9.6 20.4 all-reduce.14
  73.3 14.4 all-reduce.16
where the time goes:
time: 137 us; the launch traced here: 136 us
  waiting for transfers between devices  49.5 us (36%)
  other arithmetic  23.8 us (17%)
  blocking collectives  20.2 us (15%)
  between operations  14.3 us (10%)
  local copies, waits for them, and re-layouts  14.1 us (10%)
  starting transfers between devices  13.8 us (10%)
    psum x2, waiting for transfers between devices, pseudo_planes(): blend = lax.psum(own, 'vessel').astype(jnp.float32)  35.9 us
    all_to_all x2, blocking collectives, per_device(): lax.all_to_all(filtered, 'gather', split_axis=1, concat_axis=2, tiled=True)  20.2 us
    all_to_all x2, starting transfers between devices, per_device(): lax.all_to_all(planes, 'gather', split_axis=2, concat_axis=1, tiled=True)[0]  13.8 us
    all_to_all x2, waiting for transfers between devices, per_device(): lax.all_to_all(planes, 'gather', split_axis=2, concat_axis=1, tiled=True)[0]  13.6 us
    reduce_sum x8, other arithmetic, channel(): return (carry + jnp.sum(back, axis=0), None)  7.3 us
    unnamed x26, local copies, waits for them, and re-layouts  5.08 us
    unnamed x8, other arithmetic  4.17 us
    sub x8, other arithmetic, channel(): shrunk = forward_pass - jnp.clip(forward_pass, -bound, bound)  4.06 us
  transfers between devices with their start and end apart: 4, of which 4 were waited for; matrix products, arithmetic and copies ran while one was open for 0% of the time, Pallas kernels for 0%

commit v1 on v0

v1 whole, which is shorter than its diff:
```python
import functools

import jax
import jax.numpy as jnp
from jax import lax
from jax.experimental import pallas as pl
from jax.experimental.pallas import tpu as pltpu
from jax.sharding import PartitionSpec as P

TIME_SPACING = 4
SHOT_SPACING = 2
MAXD = 256
ITERS = 2
LANES = 128
REACH = 3

MESH = pl.DeviceIdType.MESH


def shift_left(padded, amount, width, top):
    current = padded
    step = top
    keep = top
    while step >= LANES:
        bit = (amount & step) != 0
        current = jnp.where(bit, current[:, step : step + width + keep], current[:, : width + keep])
        step //= 2
        keep = step
    extent = width + LANES
    current = current[:, :extent]
    while step >= 1:
        bit = (amount & step) != 0
        current = jnp.where(bit, pltpu.roll(current, extent - step, 1), current)
        step //= 2
    return current[:, :width]


def kernel(
    dims,
    x_ref,
    obs_ref,
    d_ref,
    tt_ref,
    ts_ref,
    th_ref,
    out_ref,
    flat,
    flat2,
    stage,
    rbuf,
    dsend,
    drecv,
    m_s,
    mt_s,
    th_s,
    pst,
    g_s,
    tail_s,
    tail_r,
    stage2,
    rbuf2,
    s_pay,
    r_pay,
    s_del,
    r_del,
    s_tail,
    r_tail,
    s_out,
    r_out,
):
    n, width, channels, taps, chunks, rows, depth = dims
    v = lax.axis_index("vessel")
    me = lax.axis_index("gather")
    other = 1 - v
    nt = width // LANES
    group = rows // n

    barrier = pltpu.get_barrier_semaphore()

    def greet(i, carry):
        p = lax.rem(me + i, n)
        pl.semaphore_signal(barrier, inc=1, device_id=(v, p), device_id_type=MESH)
        pl.semaphore_signal(barrier, inc=1, device_id=(other, p), device_id_type=MESH)
        return carry

    lax.fori_loop(1, n, greet, 0)
    pl.semaphore_signal(barrier, inc=1, device_id=(other, me), device_id_type=MESH)

    def to_rows(ref, value):
        for i in range(nt):
            ref[pl.ds(i, n, stride=nt), :] = value[:, i * LANES : (i + 1) * LANES]

    def from_rows(ref):
        return jnp.concatenate([ref[pl.ds(i, n, stride=nt), :] for i in range(nt)], axis=1)

    to_rows(flat, x_ref[0, 0].astype(jnp.float32))
    to_rows(flat2, obs_ref[0].astype(jnp.float32))
    stage[:, 0] = flat[...].reshape(n, nt, LANES).astype(jnp.bfloat16)
    stage[:, 1] = flat2[...].reshape(n, nt, LANES).astype(jnp.bfloat16)
    dsend[...] = jnp.broadcast_to(d_ref[...], (1, LANES))

    pl.semaphore_wait(barrier, 2 * n - 1)

    def payload(p, send_at, recv_at, slot):
        return pltpu.make_async_remote_copy(
            src_ref=stage.at[p],
            dst_ref=rbuf.at[slot],
            send_sem=s_pay.at[send_at],
            recv_sem=r_pay.at[recv_at],
            device_id=(v, p),
            device_id_type=MESH,
        )

    def delay(to_vessel, p, side, send_at, vessel_at, shot_at):
        return pltpu.make_async_remote_copy(
            src_ref=dsend,
            dst_ref=drecv.at[vessel_at, shot_at],
            send_sem=s_del.at[side, send_at],
            recv_sem=r_del.at[vessel_at, shot_at],
            device_id=(to_vessel, p),
            device_id_type=MESH,
        )

    delay(other, me, 1, 0, v, me).start()

    def send(i, carry):
        p = lax.rem(me + i, n)
        payload(p, i, me, me).start()
        delay(v, p, 0, i, v, me).start()
        delay(other, p, 1, i, v, me).start()
        return carry

    lax.fori_loop(1, n, send, 0)
    rbuf[me] = stage[me]
    drecv[v, me] = dsend[...]

    def build(q, carry):
        row_ch = q * group + lax.broadcasted_iota(jnp.int32, (rows, channels), 0) // n
        pick = row_ch == lax.broadcasted_iota(jnp.int32, (rows, channels), 1)
        pick_f = pick.astype(jnp.float32)
        tt = jnp.dot(pick_f, tt_ref[...], precision=lax.Precision.HIGHEST, preferred_element_type=jnp.float32)
        ts = jnp.dot(pick_f, ts_ref[...], precision=lax.Precision.HIGHEST, preferred_element_type=jnp.float32)
        th_s[q] = jnp.sum(jnp.where(pick, th_ref[...], 0.0), axis=1, keepdims=True)
        col = lax.broadcasted_iota(jnp.int32, (rows, depth), 1)
        row = lax.broadcasted_iota(jnp.int32, (rows, depth), 0)
        apart = lax.rem(col, n) - lax.rem(row, n)
        tap_of = col // n
        a = jnp.zeros((rows, depth), jnp.float32)
        b = jnp.zeros((rows, depth), jnp.float32)
        for k in range(taps):
            a = jnp.where(tap_of == k, tt[:, k : k + 1], a)
            b = jnp.where(apart == (k - REACH) * SHOT_SPACING, ts[:, k : k + 1], b)
        m = a * b
        m_s[q] = m.astype(jnp.bfloat16)
        mt_s[q] = m.T.astype(jnp.bfloat16)
        return carry

    if chunks == 1:
        build(0, 0)
    else:
        lax.fori_loop(0, chunks, build, 0)
    if depth > taps * n:
        pst[taps * n :, :] = jnp.zeros((depth - taps * n, width), jnp.bfloat16)

    def arrive(i, carry):
        p = lax.rem(me + i, n)
        payload(p, i, p, p).wait_recv()
        delay(v, p, 0, i, v, p).wait_recv()
        delay(v, p, 0, i, other, p).wait_recv()
        return carry

    delay(other, me, 1, 0, other, me).wait_recv()
    lax.fori_loop(1, n, arrive, 0)

    flat[...] = rbuf[:, 0].astype(jnp.float32).reshape(n * nt, LANES)
    flat2[...] = rbuf[:, 1].astype(jnp.float32).reshape(n * nt, LANES)
    held = from_rows(flat)
    observed = from_rows(flat2)
    d_mine = drecv[v].reshape(n, LANES)[:, :1]
    d_other = drecv[other].reshape(n, LANES)[:, :1]

    early_mark = width - 2 * MAXD
    blocks = [(0, early_mark), (early_mark, width)]
    block_width = 512

    def filter_columns(start, stop):
        def one(q, first):
            for c0 in range(start, stop, block_width):
                c1 = min(c0 + block_width, stop)
                y = jnp.dot(m_s[q], pst[:, c0:c1], preferred_element_type=jnp.float32)
                th = th_s[q]
                z = (y - jnp.minimum(jnp.maximum(y, -th), th)).astype(jnp.bfloat16)
                g = jnp.dot(mt_s[q], z, preferred_element_type=jnp.float32)
                if first:
                    g_s[:, c0:c1] = g
                else:
                    g_s[:, c0:c1] += g

        one(0, True)
        if chunks > 1:

            def more(q, carry):
                one(q, False)
                return carry

            lax.fori_loop(1, chunks, more, 0)

    def stack_taps(piece, lead, start, stop):
        extent = piece.shape[1]
        for k in range(taps):
            step = (k - REACH) * TIME_SPACING
            moved = piece if step == 0 else pltpu.roll(piece, (extent - step) % extent, 1)
            pst[k * n : (k + 1) * n, start:stop] = moved[:, lead : lead + stop - start].astype(jnp.bfloat16)

    zeros = lambda w: jnp.zeros((n, w), jnp.float32)

    def tail_copy(it):
        return pltpu.make_async_remote_copy(
            src_ref=tail_s.at[it],
            dst_ref=tail_r.at[it],
            send_sem=s_tail.at[it],
            recv_sem=r_tail.at[it],
            device_id=(other, me),
            device_id_type=MESH,
        )

    for it in range(ITERS):
        d_held, d_plane = (d_mine, d_other) if it % 2 == 0 else (d_other, d_mine)
        tail_s[it] = held[:, width - MAXD :].astype(jnp.bfloat16)
        tail_copy(it).start()
        seen = shift_left(jnp.concatenate([observed, zeros(2 * MAXD)], axis=1), d_plane, width, MAXD)
        crossed = shift_left(
            jnp.concatenate([zeros(MAXD), held, zeros(3 * MAXD)], axis=1),
            d_plane - d_held + MAXD,
            width,
            2 * MAXD,
        )
        plane = seen - crossed
        stack_taps(
            jnp.concatenate([plane[:, : early_mark + LANES], zeros(LANES)], axis=1), 0, 0, early_mark
        )
        filter_columns(0, early_mark)
        tail_copy(it).wait_recv()
        cut = width - MAXD
        time = cut + lax.broadcasted_iota(jnp.int32, (n, MAXD), 1)
        end = jnp.where(time + d_plane < width, plane[:, cut:], tail_r[it].astype(jnp.float32))
        stack_taps(
            jnp.concatenate([plane[:, early_mark - LANES : cut], end, zeros(LANES)], axis=1),
            LANES,
            early_mark,
            width,
        )
        filter_columns(early_mark, width)
        total = zeros(width)
        for k in range(taps):
            step = (k - REACH) * TIME_SPACING
            g = g_s[k * n : (k + 1) * n, :]
            if step != 0:
                extent = width + LANES
                g = pltpu.roll(jnp.concatenate([g, zeros(LANES)], axis=1), step % extent, 1)[:, :width]
            total = total + g
        held = total.astype(jnp.bfloat16).astype(jnp.float32)

    to_rows(flat, held)
    stage2[...] = flat[...].reshape(n, nt, LANES).astype(jnp.bfloat16)

    def result(p, send_at, recv_at, slot):
        return pltpu.make_async_remote_copy(
            src_ref=stage2.at[p],
            dst_ref=rbuf2.at[slot],
            send_sem=s_out.at[send_at],
            recv_sem=r_out.at[recv_at],
            device_id=(v, p),
            device_id_type=MESH,
        )

    def send_back(i, carry):
        p = lax.rem(me + i, n)
        result(p, i, me, me).start()
        return carry

    lax.fori_loop(1, n, send_back, 0)
    rbuf2[me] = stage2[me]

    def sent(i, carry):
        p = lax.rem(me + i, n)
        payload(p, i, p, p).wait_send()
        delay(v, p, 0, i, v, p).wait_send()
        delay(other, p, 1, i, v, p).wait_send()
        return carry

    delay(other, me, 1, 0, v, me).wait_send()
    lax.fori_loop(1, n, sent, 0)
    for it in range(ITERS):
        tail_copy(it).wait_send()

    def back(i, carry):
        p = lax.rem(me + i, n)
        result(p, i, p, p).wait_recv()
        result(p, i, p, p).wait_send()
        return carry

    lax.fori_loop(1, n, back, 0)
    flat[...] = rbuf2[...].astype(jnp.float32).reshape(n * nt, LANES)
    out_ref[0, 0] = from_rows(flat).astype(jnp.bfloat16)


def per_device(n, observed, estimate, delays, taps_time, taps_shot, thresh):
    receivers, width = observed.shape[1:]
    channels, taps = taps_time.shape
    assert observed.shape[0] == 1 and receivers == n and width % LANES == 0
    group = max(1, min(channels, 256 // n))
    chunks = channels // group
    rows = group * n
    depth = -(-taps * n // LANES) * LANES
    nt = width // LANES
    bf16, f32 = jnp.bfloat16, jnp.float32
    vmem = pl.BlockSpec(memory_space=pltpu.VMEM)
    dma = pltpu.SemaphoreType.DMA
    return pl.pallas_call(
        functools.partial(kernel, (n, width, channels, taps, chunks, rows, depth)),
        out_shape=jax.ShapeDtypeStruct(estimate.shape, bf16),
        in_specs=[vmem] * 6,
        out_specs=vmem,
        scratch_shapes=[
            pltpu.VMEM((n * nt, LANES), f32),
            pltpu.VMEM((n * nt, LANES), f32),
            pltpu.VMEM((n, 2, nt, LANES), bf16),
            pltpu.VMEM((n, 2, nt, LANES), bf16),
            pltpu.VMEM((1, LANES), jnp.int32),
            pltpu.VMEM((2, n, 1, LANES), jnp.int32),
            pltpu.VMEM((chunks, rows, depth), bf16),
            pltpu.VMEM((chunks, depth, rows), bf16),
            pltpu.VMEM((chunks, rows, 1), f32),
            pltpu.VMEM((depth, width), bf16),
            pltpu.VMEM((depth, width), f32),
            pltpu.VMEM((ITERS, n, MAXD), bf16),
            pltpu.VMEM((ITERS, n, MAXD), bf16),
            pltpu.VMEM((n, nt, LANES), bf16),
            pltpu.VMEM((n, nt, LANES), bf16),
            dma((n,)),
            dma((n,)),
            dma((2, n)),
            dma((2, n)),
            dma((ITERS,)),
            dma((ITERS,)),
            dma((n,)),
            dma((n,)),
        ],
        compiler_params=pltpu.CompilerParams(collective_id=0, has_side_effects=True),
    )(estimate, observed, delays, taps_time, taps_shot, thresh.reshape(1, channels))


def solution(mesh):
    return jax.shard_map(
        functools.partial(per_device, mesh.shape["gather"]),
        mesh=mesh,
        in_specs=(
            P("gather", None, None),
            P("vessel", "gather", None, None),
            P("vessel", "gather"),
            P(),
            P(),
            P(),
        ),
        out_specs=P("vessel", "gather", None, None),
        check_vma=False,
    )
```

time: 137 us -> 31.6 us (0.23)
  waiting for transfers between devices: 49.5 us -> 0 us
  Pallas kernels: 0 us -> 27.1 us
  other arithmetic: 23.8 us -> 0 us
  blocking collectives: 20.2 us -> 0 us
  starting transfers between devices: 13.8 us -> 0 us
  between operations: 14.3 us -> 0.67 us
  local copies, waits for them, and re-layouts: 14.1 us -> 3.52 us
    psum x2 -> x0, waiting for transfers between devices: 35.9 us -> none  [pseudo_planes(): blend = lax.psum(own, 'vessel').astype(jnp.float32)]
    pallas_call x0 -> x1, Pallas kernels: none -> 27.1 us  [per_device(): pl.pallas_call(functools.partial(kernel, (n, width, channels, taps, chunk...]
    all_to_all x2 -> x0, blocking collectives: 20.2 us -> none  [per_device(): lax.all_to_all(filtered, 'gather', split_axis=1, concat_axis=2, tiled=True)]
    all_to_all x2 -> x0, starting transfers between devices: 13.8 us -> none  [per_device(): lax.all_to_all(planes, 'gather', split_axis=2, concat_axis=1, tiled=True)[0]]
    all_to_all x2 -> x0, waiting for transfers between devices: 13.6 us -> none  [per_device(): lax.all_to_all(planes, 'gather', split_axis=2, concat_axis=1, tiled=True)[0]]
    reduce_sum x8 -> x0, other arithmetic: 7.3 us -> none  [channel(): return (carry + jnp.sum(back, axis=0), None)]
    add x24 -> x0, other arithmetic: 6.15 us -> none  [the longest x8 3.48 us: along_shots(): total + taps[:, tap_index + 3][:, None, None, None] * padded[:, start_off...]
    sub x10 -> x0, other arithmetic: 5.77 us -> none  [the longest x8 4.06 us: channel(): shrunk = forward_pass - jnp.clip(forward_pass, -bound, bound)]
  transfers between devices with their start and end apart: 4 -> 0, of which waited for: 4 -> 0; matrix products, arithmetic and copies ran while one was open for 0% -> 0% of each run, Pallas kernels for 0% -> 0%
where the time goes in v1:
time: 31.6 us; the launch traced here: 31.3 us
  Pallas kernels  27.1 us (86%)
  local copies, waits for them, and re-layouts  3.52 us (11%)
  between operations  0.67 us (2%)
    pallas_call x1, Pallas kernels, per_device(): pl.pallas_call(functools.partial(kernel, (n, width, channels, taps, chunk...  27.1 us
    unnamed x5, local copies, waits for them, and re-layouts  3.52 us

profile of v1, /device:TPU:0, one launch (start us, length us, event | category | flops | bytes accessed | tf_op | source)
XLA Modules:
  0.0 31.3 jit_solution(17638431235279488502)
XLA Ops:
  0.7 0.0 copy-start
  0.7 1.4 %copy.7.tt_ref = f32[16,7]{1,0:T(8,128)} copy(f32[16,7]{0,1:T(8,128)} %param.9) | data formatting | bytes 896 | tf_op args[3]
  2.0 0.0 copy-done
  2.0 0.7 %copy.8.ts_ref = f32[16,7]{1,0:T(8,128)} copy(f32[16,7]{0,1:T(8,128)S(1)} %copy-done) | data formatting | bytes 896 | tf_op args[4]
  2.7 27.1 %shard_map.64 = bf16[1,1,16,2048]{3,2,1,0:T(8,128)(2,1)} custom-call(bf16[1,1,16,2048]{3,2,1,0:T(8,128)(2,1)} %x_ref.1, bf16[1,16,2048]{2,1,0:T(8,128)(2,1)} %obs_ref.1, s32[1,1]{1,0:T(1,128)S(6)} %copy.10.d_ref, f32[16,7]{1,0:T(8,128)} %copy.7.tt_ref, f32[16,7]{1,0:T(8,128)} %copy.8.ts_ref, f32[1,16]{1,0:T(1,128)} %bitcast.1), custom_call_target="tpu_custom_call" | custom-call | tf_op jit(solution)/shard_map/pallas_call | solution.py:320
  29.9 1.5 %copy.11 = bf16[1,1,16,2048]{3,2,1,0:T(8,128)(2,1)} copy(bf16[1,1,16,2048]{3,2,1,0:T(8,128)(2,1)} %shard_map.64) | data formatting | bytes 131072
Async XLA Ops:
  0.7 1.4 %copy-start = (f32[16,7]{0,1:T(8,128)S(1)}, f32[16,7]{0,1:T(8,128)}, u32[]{:S(2)}) copy-start(f32[16,7]{0,1:T(8,128)} %param.10) | copy-start | bytes 1348

commit v2 on v1

--- a/solution.py
+++ b/solution.py
@@ -17,19 +17,27 @@
 MESH = pl.DeviceIdType.MESH
 
 
+def across(column, extent):
+    return jnp.concatenate([column] * (extent // LANES), axis=1)
+
+
 def shift_left(padded, amount, width, top):
+    def bit_of(step, extent):
+        bit = ((amount & step) != 0).astype(jnp.float32).astype(jnp.bfloat16)
+        return across(bit, extent) > 0
+
     current = padded
     step = top
     keep = top
     while step >= LANES:
-        bit = (amount & step) != 0
+        bit = bit_of(step, width + keep)
         current = jnp.where(bit, current[:, step : step + width + keep], current[:, : width + keep])
         step //= 2
         keep = step
     extent = width + LANES
     current = current[:, :extent]
     while step >= 1:
-        bit = (amount & step) != 0
+        bit = bit_of(step, extent)
         current = jnp.where(bit, pltpu.roll(current, extent - step, 1), current)
         step //= 2
     return current[:, :width]
@@ -37,13 +45,20 @@
 
 def kernel(
     dims,
+    x_hbm,
+    obs_hbm,
+    d_hbm,
+    tt_hbm,
+    ts_hbm,
+    th_hbm,
+    out_ref,
     x_ref,
     obs_ref,
     d_ref,
     tt_ref,
     ts_ref,
     th_ref,
-    out_ref,
+    s_in,
     flat,
     flat2,
     stage,
@@ -86,6 +101,24 @@
     lax.fori_loop(1, n, greet, 0)
     pl.semaphore_signal(barrier, inc=1, device_id=(other, me), device_id_type=MESH)
 
+    loads = [
+        pltpu.make_async_copy(source, target, s_in.at[i])
+        for i, (source, target) in enumerate(
+            (
+                (x_hbm, x_ref),
+                (obs_hbm, obs_ref),
+                (d_hbm, d_ref),
+                (tt_hbm, tt_ref),
+                (ts_hbm, ts_ref),
+                (th_hbm, th_ref),
+            )
+        )
+    ]
+    for load in loads:
+        load.start()
+    for load in loads[:3]:
+        load.wait()
+
     def to_rows(ref, value):
         for i in range(nt):
             ref[pl.ds(i, n, stride=nt), :] = value[:, i * LANES : (i + 1) * LANES]
@@ -134,13 +167,16 @@
     rbuf[me] = stage[me]
     drecv[v, me] = dsend[...]
 
+    for load in loads[3:]:
+        load.wait()
+
     def build(q, carry):
         row_ch = q * group + lax.broadcasted_iota(jnp.int32, (rows, channels), 0) // n
         pick = row_ch == lax.broadcasted_iota(jnp.int32, (rows, channels), 1)
         pick_f = pick.astype(jnp.float32)
-        tt = jnp.dot(pick_f, tt_ref[...], precision=lax.Precision.HIGHEST, preferred_element_type=jnp.float32)
-        ts = jnp.dot(pick_f, ts_ref[...], precision=lax.Precision.HIGHEST, preferred_element_type=jnp.float32)
-        th_s[q] = jnp.sum(jnp.where(pick, th_ref[...], 0.0), axis=1, keepdims=True)
+        tt = lax.dot_general(pick_f, tt_ref[...], (((1,), (1,)), ((), ())), precision=lax.Precision.HIGHEST, preferred_element_type=jnp.float32)
+        ts = lax.dot_general(pick_f, ts_ref[...], (((1,), (1,)), ((), ())), precision=lax.Precision.HIGHEST, preferred_element_type=jnp.float32)
+        th_s[q] = jnp.broadcast_to(jnp.sum(jnp.where(pick, th_ref[...], 0.0), axis=1, keepdims=True), (rows, LANES))
         col = lax.broadcasted_iota(jnp.int32, (rows, depth), 1)
         row = lax.broadcasted_iota(jnp.int32, (rows, depth), 0)
         apart = lax.rem(col, n) - lax.rem(row, n)
@@ -174,21 +210,20 @@
 
     flat[...] = rbuf[:, 0].astype(jnp.float32).reshape(n * nt, LANES)
     flat2[...] = rbuf[:, 1].astype(jnp.float32).reshape(n * nt, LANES)
-    held = from_rows(flat)
-    observed = from_rows(flat2)
-    d_mine = drecv[v].reshape(n, LANES)[:, :1]
-    d_other = drecv[other].reshape(n, LANES)[:, :1]
+    held = from_rows(flat).astype(jnp.bfloat16)
+    observed = from_rows(flat2).astype(jnp.bfloat16)
+    d_mine = drecv[v].reshape(n, LANES)
+    d_other = drecv[other].reshape(n, LANES)
 
     early_mark = width - 2 * MAXD
-    blocks = [(0, early_mark), (early_mark, width)]
-    block_width = 512
+    block_width = 2048
 
     def filter_columns(start, stop):
         def one(q, first):
             for c0 in range(start, stop, block_width):
                 c1 = min(c0 + block_width, stop)
                 y = jnp.dot(m_s[q], pst[:, c0:c1], preferred_element_type=jnp.float32)
-                th = th_s[q]
+                th = across(th_s[q], c1 - c0)
                 z = (y - jnp.minimum(jnp.maximum(y, -th), th)).astype(jnp.bfloat16)
                 g = jnp.dot(mt_s[q], z, preferred_element_type=jnp.float32)
                 if first:
@@ -210,9 +245,9 @@
         for k in range(taps):
             step = (k - REACH) * TIME_SPACING
             moved = piece if step == 0 else pltpu.roll(piece, (extent - step) % extent, 1)
-            pst[k * n : (k + 1) * n, start:stop] = moved[:, lead : lead + stop - start].astype(jnp.bfloat16)
-
-    zeros = lambda w: jnp.zeros((n, w), jnp.float32)
+            pst[k * n : (k + 1) * n, start:stop] = moved[:, lead : lead + stop - start]
+
+    zeros = lambda w, t=jnp.bfloat16: jnp.zeros((n, w), t)
 
     def tail_copy(it):
         return pltpu.make_async_remote_copy(
@@ -226,7 +261,7 @@
 
     for it in range(ITERS):
         d_held, d_plane = (d_mine, d_other) if it % 2 == 0 else (d_other, d_mine)
-        tail_s[it] = held[:, width - MAXD :].astype(jnp.bfloat16)
+        tail_s[it] = held[:, width - MAXD :]
         tail_copy(it).start()
         seen = shift_left(jnp.concatenate([observed, zeros(2 * MAXD)], axis=1), d_plane, width, MAXD)
         crossed = shift_left(
@@ -235,7 +270,8 @@
             width,
             2 * MAXD,
         )
-        plane = seen - crossed
+        exact = seen.astype(jnp.float32) - crossed.astype(jnp.float32)
+        plane = exact.astype(jnp.bfloat16)
         stack_taps(
             jnp.concatenate([plane[:, : early_mark + LANES], zeros(LANES)], axis=1), 0, 0, early_mark
         )
@@ -243,7 +279,8 @@
         tail_copy(it).wait_recv()
         cut = width - MAXD
         time = cut + lax.broadcasted_iota(jnp.int32, (n, MAXD), 1)
-        end = jnp.where(time + d_plane < width, plane[:, cut:], tail_r[it].astype(jnp.float32))
+        end = jnp.where(time + across(d_plane, MAXD) < width, exact[:, cut:], tail_r[it].astype(jnp.float32))
+        end = end.astype(jnp.bfloat16)
         stack_taps(
             jnp.concatenate([plane[:, early_mark - LANES : cut], end, zeros(LANES)], axis=1),
             LANES,
@@ -251,17 +288,17 @@
             width,
         )
         filter_columns(early_mark, width)
-        total = zeros(width)
+        total = zeros(width, jnp.float32)
         for k in range(taps):
             step = (k - REACH) * TIME_SPACING
             g = g_s[k * n : (k + 1) * n, :]
             if step != 0:
                 extent = width + LANES
-                g = pltpu.roll(jnp.concatenate([g, zeros(LANES)], axis=1), step % extent, 1)[:, :width]
+                g = pltpu.roll(jnp.concatenate([g, zeros(LANES, jnp.float32)], axis=1), step % extent, 1)[:, :width]
             total = total + g
-        held = total.astype(jnp.bfloat16).astype(jnp.float32)
-
-    to_rows(flat, held)
+        held = total.astype(jnp.bfloat16)
+
+    to_rows(flat, held.astype(jnp.float32))
     stage2[...] = flat[...].reshape(n, nt, LANES).astype(jnp.bfloat16)
 
     def result(p, send_at, recv_at, slot):
@@ -320,9 +357,16 @@
     return pl.pallas_call(
         functools.partial(kernel, (n, width, channels, taps, chunks, rows, depth)),
         out_shape=jax.ShapeDtypeStruct(estimate.shape, bf16),
-        in_specs=[vmem] * 6,
+        in_specs=[pl.BlockSpec(memory_space=pl.ANY)] * 6,
         out_specs=vmem,
         scratch_shapes=[
+            pltpu.VMEM((1, 1, n, width), bf16),
+            pltpu.VMEM((1, n, width), bf16),
+            pltpu.VMEM((1, 1), jnp.int32),
+            pltpu.VMEM((taps, channels), f32),
+            pltpu.VMEM((taps, channels), f32),
+            pltpu.VMEM((1, channels), f32),
+            dma((6,)),
             pltpu.VMEM((n * nt, LANES), f32),
             pltpu.VMEM((n * nt, LANES), f32),
             pltpu.VMEM((n, 2, nt, LANES), bf16),
@@ -331,7 +375,7 @@
             pltpu.VMEM((2, n, 1, LANES), jnp.int32),
             pltpu.VMEM((chunks, rows, depth), bf16),
             pltpu.VMEM((chunks, depth, rows), bf16),
-            pltpu.VMEM((chunks, rows, 1), f32),
+            pltpu.VMEM((chunks, rows, LANES), f32),
             pltpu.VMEM((depth, width), bf16),
             pltpu.VMEM((depth, width), f32),
             pltpu.VMEM((ITERS, n, MAXD), bf16),
@@ -348,7 +392,7 @@
             dma((n,)),
         ],
         compiler_params=pltpu.CompilerParams(collective_id=0, has_side_effects=True),
-    )(estimate, observed, delays, taps_time, taps_shot, thresh.reshape(1, channels))
+    )(estimate, observed, delays, taps_time.T, taps_shot.T, thresh.reshape(1, channels))
 
 
 def solution(mesh):

time: 31.6 us -> 26.1 us (0.83)
  Pallas kernels: 27.1 us -> 23.7 us
  local copies, waits for them, and re-layouts: 3.52 us -> 1.47 us
    pallas_call x1, Pallas kernels: 27.1 us -> 23.7 us  [per_device(): pl.pallas_call(functools.partial(kernel, (n, width, channels, taps, chunk...]
    unnamed x5 -> x1, local copies, waits for them, and re-layouts: 3.52 us -> 1.47 us
where the time goes in v2:
time: 26.1 us; the launch traced here: 25.9 us
  Pallas kernels  23.7 us (91%)
  local copies, waits for them, and re-layouts  1.47 us (6%)
  between operations  0.66 us (3%)
    pallas_call x1, Pallas kernels, per_device(): pl.pallas_call(functools.partial(kernel, (n, width, channels, taps, chunk...  23.7 us
    unnamed x1, local copies, waits for them, and re-layouts  1.47 us

profile of v2, /device:TPU:0, one launch (start us, length us, event | category | flops | bytes accessed | tf_op | source)
XLA Modules:
  0.0 25.9 jit_solution(13687197585337721829)
XLA Ops:
  0.7 23.7 %shard_map.64 = bf16[1,1,16,2048]{3,2,1,0:T(8,128)(2,1)} custom-call(bf16[1,1,16,2048]{3,2,1,0:T(8,128)(2,1)} %x_hbm.1, bf16[1,16,2048]{2,1,0:T(8,128)(2,1)} %obs_hbm.1, s32[1,1]{1,0:T(1,128)S(6)} %copy.8.d_hbm, f32[7,16]{1,0:T(8,128)} %bitcast.3, f32[7,16]{1,0:T(8,128)} %bitcast.4, f32[1,16]{1,0:T(1,128)} %bitcast.5), custom_call_target="tpu_custom_call" | custom-call | tf_op jit(solution)/shard_map/pallas_call | solution.py:357
  24.4 1.5 %copy.9 = bf16[1,1,16,2048]{3,2,1,0:T(8,128)(2,1)} copy(bf16[1,1,16,2048]{3,2,1,0:T(8,128)(2,1)} %shard_map.64) | data formatting | bytes 131072

commit v3 on v2

--- a/solution.py
+++ b/solution.py
@@ -17,28 +17,33 @@
 MESH = pl.DeviceIdType.MESH
 
 
+def partner_of(me, i, n):
+    return me ^ (n - i) if n & (n - 1) == 0 else lax.rem(me + i, n)
+
+
 def across(column, extent):
     return jnp.concatenate([column] * (extent // LANES), axis=1)
 
 
 def shift_left(padded, amount, width, top):
-    def bit_of(step, extent):
-        bit = ((amount & step) != 0).astype(jnp.float32).astype(jnp.bfloat16)
-        return across(bit, extent) > 0
+    def choose(step, moved, kept):
+        bit = ((amount & step) != 0).astype(jnp.float32)
+        extent = moved.shape[1]
+        taken = across(bit.astype(jnp.bfloat16), extent)
+        left = across((1.0 - bit).astype(jnp.bfloat16), extent)
+        return moved * taken + kept * left
 
     current = padded
     step = top
     keep = top
     while step >= LANES:
-        bit = bit_of(step, width + keep)
-        current = jnp.where(bit, current[:, step : step + width + keep], current[:, : width + keep])
+        current = choose(step, current[:, step : step + width + keep], current[:, : width + keep])
         step //= 2
         keep = step
     extent = width + LANES
     current = current[:, :extent]
     while step >= 1:
-        bit = bit_of(step, extent)
-        current = jnp.where(bit, pltpu.roll(current, extent - step, 1), current)
+        current = choose(step, pltpu.roll(current, extent - step, 1), current)
         step //= 2
     return current[:, :width]
 
@@ -154,16 +159,20 @@
             device_id_type=MESH,
         )
 
-    delay(other, me, 1, 0, v, me).start()
-
     def send(i, carry):
-        p = lax.rem(me + i, n)
+        p = partner_of(me, i, n)
         payload(p, i, me, me).start()
+        return carry
+
+    def send_delay(i, carry):
+        p = partner_of(me, i, n)
         delay(v, p, 0, i, v, me).start()
         delay(other, p, 1, i, v, me).start()
         return carry
 
     lax.fori_loop(1, n, send, 0)
+    lax.fori_loop(1, n, send_delay, 0)
+    delay(other, me, 1, 0, v, me).start()
     rbuf[me] = stage[me]
     drecv[v, me] = dsend[...]
 
@@ -199,7 +208,7 @@
         pst[taps * n :, :] = jnp.zeros((depth - taps * n, width), jnp.bfloat16)
 
     def arrive(i, carry):
-        p = lax.rem(me + i, n)
+        p = partner_of(me, i, n)
         payload(p, i, p, p).wait_recv()
         delay(v, p, 0, i, v, p).wait_recv()
         delay(v, p, 0, i, other, p).wait_recv()
@@ -312,7 +321,7 @@
         )
 
     def send_back(i, carry):
-        p = lax.rem(me + i, n)
+        p = partner_of(me, i, n)
         result(p, i, me, me).start()
         return carry
 
@@ -320,7 +329,7 @@
     rbuf2[me] = stage2[me]
 
     def sent(i, carry):
-        p = lax.rem(me + i, n)
+        p = partner_of(me, i, n)
         payload(p, i, p, p).wait_send()
         delay(v, p, 0, i, v, p).wait_send()
         delay(other, p, 1, i, v, p).wait_send()
@@ -332,7 +341,7 @@
         tail_copy(it).wait_send()
 
     def back(i, carry):
-        p = lax.rem(me + i, n)
+        p = partner_of(me, i, n)
         result(p, i, p, p).wait_recv()
         result(p, i, p, p).wait_send()
         return carry
@@ -354,9 +363,14 @@
     bf16, f32 = jnp.bfloat16, jnp.float32
     vmem = pl.BlockSpec(memory_space=pltpu.VMEM)
     dma = pltpu.SemaphoreType.DMA
+    operands = (estimate, observed, delays, taps_time.T, taps_shot.T, thresh.reshape(1, channels))
+    operands = [
+        operand if operand is delays else pltpu.with_memory_space_constraint(operand, pltpu.HBM)
+        for operand in operands
+    ]
     return pl.pallas_call(
         functools.partial(kernel, (n, width, channels, taps, chunks, rows, depth)),
-        out_shape=jax.ShapeDtypeStruct(estimate.shape, bf16),
+        out_shape=pltpu.VMEM(estimate.shape, bf16),
         in_specs=[pl.BlockSpec(memory_space=pl.ANY)] * 6,
         out_specs=vmem,
         scratch_shapes=[
@@ -391,8 +405,8 @@
             dma((n,)),
             dma((n,)),
         ],
-        compiler_params=pltpu.CompilerParams(collective_id=0, has_side_effects=True),
-    )(estimate, observed, delays, taps_time.T, taps_shot.T, thresh.reshape(1, channels))
+        compiler_params=pltpu.CompilerParams(collective_id=0, has_side_effects=True, vmem_limit_bytes=48 << 20),
+        )(*operands)
 
 
 def solution(mesh):

time: 26.1 us -> 24.5 us (0.939)
  local copies, waits for them, and re-layouts: 1.47 us -> 0.63 us
  Pallas kernels: 23.7 us -> 23.1 us
    unnamed x1, local copies, waits for them, and re-layouts: 1.47 us -> 0.63 us
    pallas_call x1, Pallas kernels: 23.7 us -> 23.1 us  [per_device(): pl.pallas_call(functools.partial(kernel, (n, width, channels, taps, chunk...]
where the time goes in v3:
time: 24.5 us; the launch traced here: 24.4 us
  Pallas kernels  23.1 us (94%)
  between operations  0.66 us (3%)
  local copies, waits for them, and re-layouts  0.63 us (3%)
    pallas_call x1, Pallas kernels, per_device(): pl.pallas_call(functools.partial(kernel, (n, width, channels, taps, chunk...  23.1 us
    unnamed x1, local copies, waits for them, and re-layouts  0.63 us

profile of v3, /device:TPU:0, one launch (start us, length us, event | category | flops | bytes accessed | tf_op | source)
XLA Modules:
  0.0 24.4 jit_solution(12503158119988503366)
XLA Ops:
  0.7 23.1 %shard_map.64 = bf16[1,1,16,2048]{3,2,1,0:T(8,128)(2,1)S(1)} custom-call(bf16[1,1,16,2048]{3,2,1,0:T(8,128)(2,1)} %x_hbm.1, bf16[1,16,2048]{2,1,0:T(8,128)(2,1)} %obs_hbm.1, s32[1,1]{1,0:T(1,128)S(6)} %copy.9.d_hbm, f32[7,16]{1,0:T(8,128)} %bitcast.3, f32[7,16]{1,0:T(8,128)} %bitcast.4, f32[1,16]{1,0:T(1,128)} %bitcast.5), custom_call_target="tpu_custom_call" | custom-call | tf_op jit(solution)/shard_map/pallas_call | solution.py:371
  23.7 0.6 %copy.8 = bf16[1,1,16,2048]{3,2,1,0:T(8,128)(2,1)} copy(bf16[1,1,16,2048]{3,2,1,0:T(8,128)(2,1)S(1)} %shard_map.64) | data formatting | bytes 131072
